TPU v7x, 512 devices: a whole 4x8x8 slice. The times are simulated.
512 devices in a mesh: asset: 64 (over y, z), rhs: 8 (over x, core).
Axes of the slice: x: 4, y: 8, z: 8, core: 2. Of those that a mesh axis runs over, the one named last changes fastest.
Arguments:
- targets: float32 [65536, 1024], P('asset', 'rhs'), may hold values from -27 to 27
- ridge: float32 [65536], P('asset'), may hold values from 0.8 to 2.5
- blocks: bfloat16 [512, 16, 128, 128], P('asset', None, 'rhs'), may hold values from -0.046875 to 0.046875
- col_index: int32 [512, 16], P('asset'), may hold values from 0 to 511, as said below
- row_length: int32 [512], P('asset'), may hold values from 8 to 16, as said below
Outputs:
- solution: float32 [65536, 1024], P('asset', 'rhs')
- residual: float32 [65536, 1024], P('asset', 'rhs')
Inputs may be any that keep to these rules, and one draw needn't show every extreme that they name: `col_index`: the block columns of row i are distinct and lie within 8 blocks of i, counted cyclically modulo 512; slots at or past row_length[i] hold such columns too and are ignored. `row_length`: each aligned group of 8 block rows holds at least one row with 16 used slots.
All inputs are finite; a program needn't handle non-finite values.
Results may differ from a plain program's by a relative error of at most 0.0075.
Values may be sent and summed in bfloat16 or wider, within the bound.
A program may use at most 64 MiB of HBM per device.

v0:
```python
import jax
import jax.numpy as jnp
from jax import lax
from jax.sharding import PartitionSpec as P

ITERS = 3


def from_behind(block, axis, distance):
    devices = range(lax.axis_size(axis))
    route = [((i - distance) % len(devices), i) for i in devices]
    return lax.ppermute(block, axis, route)


def extended_2(shard, sides, width):
    for axis, dim in sides:
        devices, length = (lax.axis_size(axis), shard.shape[dim])
        up = [(i, (i + 1) % devices) for i in range(devices)]
        down = [(j, i) for i, j in up]
        last = lax.slice_in_dim(shard, length - width, length, axis=dim)
        first = lax.slice_in_dim(shard, 0, width, axis=dim)
        before = lax.ppermute(last, axis, up)
        after = lax.ppermute(first, axis, down)
        shard = jnp.concatenate([before, shard, after], axis=dim)
    return shard


def shards(targets, ridge, blocks, col_index, row_length):
    rows = col_index.shape[0]
    slots = col_index.shape[1]
    width = blocks.shape[3]
    cols = targets.shape[1]
    total = rows * lax.axis_size("asset")
    start = lax.axis_index("asset") * rows
    used = jnp.arange(slots)[None, :] < row_length[:, None]
    masked_shard = blocks * used[:, :, None, None].astype(jnp.bfloat16)
    local_pos = (col_index - start + rows) % total
    onehot = (local_pos[None, :, :] == jnp.arange(3 * rows, dtype=jnp.int32)[:, None, None]).astype(
        jnp.bfloat16
    )
    own_blocks = lax.all_gather(masked_shard, "rhs", axis=2, tiled=True)
    weave = jnp.einsum(
        "cik,ikab->ciab", onehot, own_blocks, preferred_element_type=jnp.float32
    ).astype(jnp.bfloat16)

    def squares(values):
        return lax.psum(jnp.sum(values * values, axis=0), "asset")

    solution = jnp.zeros_like(targets)
    residual = targets
    direction = targets
    norm_now = squares(residual)
    for step in range(ITERS):
        rounded = direction.astype(jnp.bfloat16)
        operate_extended = extended_2(rounded, (("asset", 0),), rows * width)
        operate_extended = operate_extended.reshape(3 * rows, width, cols)
        picked = jnp.take(operate_extended, local_pos, axis=0)
        forward = jnp.einsum(
            "ikab,ikbn->ian", own_blocks, picked, preferred_element_type=jnp.float32
        )
        slab = jnp.einsum(
            "qjpt,jpu->qtu",
            weave,
            operate_extended[rows : 2 * rows],
            preferred_element_type=jnp.float32,
        )
        from_upper = from_behind(slab[:rows].astype(jnp.bfloat16), "asset", -1).astype(jnp.float32)
        from_lower = from_behind(slab[2 * rows :].astype(jnp.bfloat16), "asset", 1).astype(
            jnp.float32
        )
        backward = slab[rows : 2 * rows] + from_upper + from_lower
        image = ridge[:, None] * direction + 0.5 * (forward + backward).reshape(rows * width, cols)
        curve = lax.psum(jnp.sum(direction * image, axis=0), "asset")
        alpha = norm_now / curve
        solution = solution + alpha * direction
        residual = residual - alpha * image
        norm_next = squares(residual)
        direction = residual + norm_next / norm_now * direction
        norm_now = norm_next
    return (solution, residual)


def solution(mesh):
    return jax.shard_map(
        shards,
        mesh=mesh,
        in_specs=(
            P("asset", "rhs"),
            P("asset"),
            P("asset", None, "rhs", None),
            P("asset", None),
            P("asset"),
        ),
        out_specs=(P("asset", "rhs"), P("asset", "rhs")),
        check_vma=False,
    )
```

profile of v0, /device:TPU:2, one launch (start us, length us, event | category | flops | bytes accessed | tf_op | source)
XLA Modules:
  0.0 876.3 jit_solution(18036171837793183966)
XLA Ops:
  11.1 13.9 %collective-permute-start.1 = (bf16[1024,128]{1,0:T(8,128)(2,1)S(1)}, bf16[1024,128]{1,0:T(8,128)(2,1)S(1)}, u32[]{:S(2)}, u32[]{:S(2)}) collective-permute-start(bf16[1024,128]{1,0:T(8,128)(2,1)S(1)} %convert_element_type.49), channel_id=1, source_target_pairs={{8,0},{16,8},{24,16},{32,24},{40,32},{48,40},{56,48},{64,56},{72,6... | collective-permute-start | bytes 786440 | tf_op jit(solution)/shard_map/ppermute | solution.py:23
  27.7 28.8 %all-gather.2.cloned.1.call-done = bf16[8,16,128,128]{3,2,1,0:T(8,128)(2,1)} async-done(((bf16[8,16,16,128]{3,2,1,0:T(8,128)(2,1)}), bf16[8,16,128,128]{3,2,1,0:T(8,128)(2,1)}) %all-gather.2.cloned.1.call-update) | async-done | bytes 4194320 | tf_op jit(solution)/shard_map/all_gather | solution.py:41
  56.4 8.0 convert_bitcast_fusion
  64.4 9.0 %copy.8 = bf16[24,8,128,128]{2,3,1,0:T(8,128)(2,1)} copy(bf16[24,8,128,128]{3,0,2,1:T(8,128)(2,1)} %convert_bitcast_fusion) | data formatting | bytes 12582912 | tf_op jit(solution)/shard_map/convert_element_type | solution.py:44
  73.5 4.6 fusion.53
  78.8 3.5 collective-permute-start.3
  82.3 6.5 collective-permute-start.2
  88.9 3.1 gather_fusion
  94.8 4.9 fusion.33
  100.0 143.9 %all-reduce = (f32[128]{0:T(128)S(1)}, f32[128]{0:T(128)S(1)}) all-reduce(f32[128]{0:T(128)S(1)} %get-tuple-element.4, f32[128]{0:T(128)S(1)} %get-tuple-element.3), channel_id=1, replica_groups=mesh['asset'=64,'rhs'=8] {'asset'}, use_global_device_ids=true, to_apply=%region_1.2 | all-reduce | flops 256 | bytes 2048 | tf_op jit(solution)/shard_map/psum | solution.py:47
  244.1 138.3 %psum.44 = f32[128]{0:T(128)S(1)} all-reduce(f32[128]{0:T(128)S(1)} %multiply_reduce_fusion.3), channel_id=1, replica_groups=mesh['asset'=64,'rhs'=8] {'asset'}, use_global_device_ids=true, to_apply=%region_5.7 | all-reduce | flops 128 | bytes 1024 | tf_op jit(solution)/shard_map/psum | solution.py:47
  382.6 3.7 collective-permute-start.5
  388.5 5.7 fusion.54
  394.3 3.7 collective-permute-start.7
  397.9 5.7 collective-permute-start.6
  407.3 4.9 fusion.30
  412.5 143.7 %psum.45 = f32[128]{0:T(128)S(1)} all-reduce(f32[128]{0:T(128)S(1)} %multiply_reduce_fusion.2), channel_id=1, replica_groups=mesh['asset'=64,'rhs'=8] {'asset'}, use_global_device_ids=true, to_apply=%region_7.9 | all-reduce | flops 128 | bytes 1024 | tf_op jit(solution)/shard_map/psum | solution.py:73
  556.5 138.0 %psum.46 = f32[128]{0:T(128)S(1)} all-reduce(f32[128]{0:T(128)S(1)} %get-tuple-element.7), channel_id=1, replica_groups=mesh['asset'=64,'rhs'=8] {'asset'}, use_global_device_ids=true, to_apply=%region_9.11 | all-reduce | flops 128 | bytes 1024 | tf_op jit(solution)/shard_map/psum | solution.py:47
  694.5 3.9 collective-permute-start.9
  700.4 5.7 fusion.55
  706.1 3.9 collective-permute-start.11
  710.1 5.3 collective-permute-start.10
  719.2 5.0 fusion.27
  724.4 143.9 %psum.47 = f32[128]{0:T(128)S(1)} all-reduce(f32[128]{0:T(128)S(1)} %multiply_reduce_fusion), channel_id=1, replica_groups=mesh['asset'=64,'rhs'=8] {'asset'}, use_global_device_ids=true, to_apply=%region_11.13 | all-reduce | flops 128 | bytes 1024 | tf_op jit(solution)/shard_map/psum | solution.py:73
  (49 shorter events, 24.5 us)
Async XLA Ops:
  7.2 49.3 %all-gather.2.cloned.1.call-start = ((), (), s32[]{:S(2)}) async-start(), calls=%async_computation | async-start | bytes 4718592 | tf_op jit(solution)/shard_map/all_gather | solution.py:41
  11.1 77.8 %collective-permute-start.1 = (bf16[1024,128]{1,0:T(8,128)(2,1)S(1)}, bf16[1024,128]{1,0:T(8,128)(2,1)S(1)}, u32[]{:S(2)}, u32[]{:S(2)}) collective-permute-start(bf16[1024,128]{1,0:T(8,128)(2,1)S(1)} %convert_element_type.49), channel_id=1, source_target_pairs={{8,0},{16,8},{24,16},{32,24},{40,32},{48,40},{56,48},{64,56},{72,6... | collective-permute-start | bytes 786440 | tf_op jit(solution)/shard_map/ppermute | solution.py:23
  24.9 63.9 %collective-permute-start = (bf16[1024,128]{1,0:T(8,128)(2,1)S(1)}, bf16[1024,128]{1,0:T(8,128)(2,1)S(1)}, u32[]{:S(2)}, u32[]{:S(2)}) collective-permute-start(bf16[1024,128]{1,0:T(8,128)(2,1)S(1)} %convert_element_type.49), channel_id=1, source_target_pairs={{0,8},{8,16},{16,24},{24,32},{32,40},{40,48},{48,56},{56,64},{64,7... | collective-permute-start | bytes 786440 | tf_op jit(solution)/shard_map/ppermute | solution.py:22
  78.8 15.2 %collective-permute-start.3 = (bf16[8,128,128]{2,1,0:T(8,128)(2,1)}, bf16[8,128,128]{2,1,0:T(8,128)(2,1)}, u32[]{:S(2)}, u32[]{:S(2)}) collective-permute-start(bf16[8,128,128]{2,1,0:T(8,128)(2,1)} %get-tuple-element.20), channel_id=1, source_target_pairs={{504,0},{0,8},{8,16},{16,24},{24,32},{32,40},{40,48},{48,56},{56,6... | collective-permute-start | bytes 786440 | tf_op jit(solution)/shard_map/ppermute | solution.py:12
  82.3 12.5 %collective-permute-start.2 = (bf16[8,128,128]{2,1,0:T(8,128)(2,1)S(1)}, bf16[8,128,128]{2,1,0:T(8,128)(2,1)}, u32[]{:S(2)}, u32[]{:S(2)}) collective-permute-start(bf16[8,128,128]{2,1,0:T(8,128)(2,1)S(1)} %get-tuple-element.19), channel_id=1, source_target_pairs={{8,0},{16,8},{24,16},{32,24},{40,32},{48,40},{56,48},{64,56},{72,6... | collective-permute-start | bytes 786440 | tf_op jit(solution)/shard_map/ppermute | solution.py:12
  94.8 4.9 copy-start
  94.8 5.0 copy-start.1
  382.6 21.0 %collective-permute-start.5 = (bf16[1024,128]{1,0:T(8,128)(2,1)S(1)}, bf16[1024,128]{1,0:T(8,128)(2,1)S(1)}, u32[]{:S(2)}, u32[]{:S(2)}) collective-permute-start(bf16[1024,128]{1,0:T(8,128)(2,1)S(1)} %get-tuple-element.9), channel_id=1, source_target_pairs={{8,0},{16,8},{24,16},{32,24},{40,32},{48,40},{56,48},{64,56},{72,6... | collective-permute-start | bytes 786440 | tf_op jit(solution)/shard_map/ppermute | solution.py:23
  386.3 17.3 %collective-permute-start.4 = (bf16[1024,128]{1,0:T(8,128)(2,1)S(1)}, bf16[1024,128]{1,0:T(8,128)(2,1)S(1)}, u32[]{:S(2)}, u32[]{:S(2)}) collective-permute-start(bf16[1024,128]{1,0:T(8,128)(2,1)S(1)} %get-tuple-element.9), channel_id=1, source_target_pairs={{0,8},{8,16},{16,24},{24,32},{32,40},{40,48},{48,56},{56,64},{64,7... | collective-permute-start | bytes 786440 | tf_op jit(solution)/shard_map/ppermute | solution.py:22
  394.3 12.6 %collective-permute-start.7 = (bf16[8,128,128]{2,1,0:T(8,128)(2,1)S(1)}, bf16[8,128,128]{2,1,0:T(8,128)(2,1)S(1)}, u32[]{:S(2)}, u32[]{:S(2)}) collective-permute-start(bf16[8,128,128]{2,1,0:T(8,128)(2,1)S(1)} %get-tuple-element.18), channel_id=1, source_target_pairs={{504,0},{0,8},{8,16},{16,24},{24,32},{32,40},{40,48},{48,56},{56,6... | collective-permute-start | bytes 786440 | tf_op jit(solution)/shard_map/ppermute | solution.py:12
  397.9 9.4 %collective-permute-start.6 = (bf16[8,128,128]{2,1,0:T(8,128)(2,1)S(1)}, bf16[8,128,128]{2,1,0:T(8,128)(2,1)S(1)}, u32[]{:S(2)}, u32[]{:S(2)}) collective-permute-start(bf16[8,128,128]{2,1,0:T(8,128)(2,1)S(1)} %get-tuple-element.17), channel_id=1, source_target_pairs={{8,0},{16,8},{24,16},{32,24},{40,32},{48,40},{56,48},{64,56},{72,6... | collective-permute-start | bytes 786440 | tf_op jit(solution)/shard_map/ppermute | solution.py:12
  694.5 20.8 %collective-permute-start.9 = (bf16[1024,128]{1,0:T(8,128)(2,1)S(1)}, bf16[1024,128]{1,0:T(8,128)(2,1)S(1)}, u32[]{:S(2)}, u32[]{:S(2)}) collective-permute-start(bf16[1024,128]{1,0:T(8,128)(2,1)S(1)} %fusion.34), channel_id=1, source_target_pairs={{8,0},{16,8},{24,16},{32,24},{40,32},{48,40},{56,48},{64,56},{72,6... | collective-permute-start | bytes 786440 | tf_op jit(solution)/shard_map/ppermute | solution.py:23
  698.4 16.9 %collective-permute-start.8 = (bf16[1024,128]{1,0:T(8,128)(2,1)S(1)}, bf16[1024,128]{1,0:T(8,128)(2,1)S(1)}, u32[]{:S(2)}, u32[]{:S(2)}) collective-permute-start(bf16[1024,128]{1,0:T(8,128)(2,1)S(1)} %fusion.34), channel_id=1, source_target_pairs={{0,8},{8,16},{16,24},{24,32},{32,40},{40,48},{48,56},{56,64},{64,7... | collective-permute-start | bytes 786440 | tf_op jit(solution)/shard_map/ppermute | solution.py:22
  706.1 12.3 %collective-permute-start.11 = (bf16[8,128,128]{2,1,0:T(8,128)(2,1)S(1)}, bf16[8,128,128]{2,1,0:T(8,128)(2,1)}, u32[]{:S(2)}, u32[]{:S(2)}) collective-permute-start(bf16[8,128,128]{2,1,0:T(8,128)(2,1)S(1)} %get-tuple-element.16), channel_id=1, source_target_pairs={{504,0},{0,8},{8,16},{16,24},{24,32},{32,40},{40,48},{48,56},{56,6... | collective-permute-start | bytes 786440 | tf_op jit(solution)/shard_map/ppermute | solution.py:12
  710.1 9.1 %collective-permute-start.10 = (bf16[8,128,128]{2,1,0:T(8,128)(2,1)S(1)}, bf16[8,128,128]{2,1,0:T(8,128)(2,1)}, u32[]{:S(2)}, u32[]{:S(2)}) collective-permute-start(bf16[8,128,128]{2,1,0:T(8,128)(2,1)S(1)} %get-tuple-element.15), channel_id=1, source_target_pairs={{8,0},{16,8},{24,16},{32,24},{40,32},{48,40},{56,48},{64,56},{72,6... | collective-permute-start | bytes 786440 | tf_op jit(solution)/shard_map/ppermute | solution.py:12
Sparse Core Ops, SparseCore 0:
  10.7 45.6 all-gather.1
where the time goes:
time: 877 us; the launch traced here: 876 us
  blocking collectives  708 us (81%)
  starting transfers between devices  56 us (6%)
  matrix products  38.9 us (4%)
  waiting for transfers between devices  32.9 us (4%)
  local copies, waits for them, and re-layouts  19.2 us (2%)
  between operations  14.3 us (2%)
    psum x3, blocking collectives, squares(): return lax.psum(jnp.sum(values * values, axis=0), 'asset')  420 us
    psum x2, blocking collectives, shards(): curve = lax.psum(jnp.sum(direction * image, axis=0), 'asset')  288 us
    all_gather x1, waiting for transfers between devices, shards(): own_blocks = lax.all_gather(masked_shard, 'rhs', axis=2, tiled=True)  28.8 us
    ppermute x6, starting transfers between devices, from_behind(): return lax.ppermute(block, axis, route)  28.5 us
    ppermute x3, starting transfers between devices, extended_2(): after = lax.ppermute(first, axis, down)  21.4 us
  transfers between devices with their start and end apart: 13, of which 5 were waited for; matrix products, arithmetic and copies ran while one was open for 5% of the time, Pallas kernels for 0%

commit v1 on v0

--- a/solution.py
+++ b/solution.py
@@ -44,7 +44,7 @@
     ).astype(jnp.bfloat16)
 
     def squares(values):
-        return lax.psum(jnp.sum(values * values, axis=0), "asset")
+        return jnp.sum(lax.all_gather(jnp.sum(values * values, axis=0), "asset"), axis=0)
 
     solution = jnp.zeros_like(targets)
     residual = targets

time: 877 us -> 721 us (0.82)
  the two profiles are of different devices: /device:TPU:2 before, /device:TPU:4 now
where the time goes in v1:
time: 721 us; the launch traced here: 720 us
  blocking collectives  550 us (76%)
  starting transfers between devices  57.3 us (8%)
  matrix products  39 us (5%)
  waiting for transfers between devices  32.9 us (5%)
  local copies, waits for them, and re-layouts  19.2 us (3%)
  between operations  14.3 us (2%)
  other arithmetic  7.59 us (1%)
    psum x3, blocking collectives, shards(): curve = lax.psum(jnp.sum(direction * image, axis=0), 'asset')  427 us
    all_gather x3, blocking collectives, squares(): lax.all_gather(jnp.sum(values * values, axis=0), 'asset')  123 us
    all_gather x1, waiting for transfers between devices, shards(): own_blocks = lax.all_gather(masked_shard, 'rhs', axis=2, tiled=True)  28.8 us
    ppermute x6, starting transfers between devices, from_behind(): return lax.ppermute(block, axis, route)  28.5 us
    ppermute x3, starting transfers between devices, extended_2(): after = lax.ppermute(first, axis, down)  22.4 us
    dot_general x3, matrix products, shards(): jnp.einsum('qjpt,jpu->qtu', weave, operate_extended[rows:2 * rows], prefe...  16 us
    dot_general x3, matrix products, shards(): jnp.einsum('ikab,ikbn->ian', own_blocks, picked, preferred_element_type=j...  14.9 us
  transfers between devices with their start and end apart: 13, of which 5 were waited for; matrix products, arithmetic and copies ran while one was open for 6% of the time, Pallas kernels for 0%

profile of v1, /device:TPU:4, one launch (start us, length us, event | category | flops | bytes accessed | tf_op | source)
XLA Modules:
  0.0 720.5 jit_solution(11352499120608561643)
XLA Ops:
  11.1 13.9 %collective-permute-start.1 = (bf16[1024,128]{1,0:T(8,128)(2,1)S(1)}, bf16[1024,128]{1,0:T(8,128)(2,1)S(1)}, u32[]{:S(2)}, u32[]{:S(2)}) collective-permute-start(bf16[1024,128]{1,0:T(8,128)(2,1)S(1)} %convert_element_type.49), channel_id=1, source_target_pairs={{8,0},{16,8},{24,16},{32,24},{40,32},{48,40},{56,48},{64,56},{72,6... | collective-permute-start | bytes 786440 | tf_op jit(solution)/shard_map/ppermute | solution.py:23
  27.7 28.8 %all-gather.8.cloned.1.call-done = bf16[8,16,128,128]{3,2,1,0:T(8,128)(2,1)} async-done(((bf16[8,16,16,128]{3,2,1,0:T(8,128)(2,1)}), bf16[8,16,128,128]{3,2,1,0:T(8,128)(2,1)}) %all-gather.8.cloned.1.call-update) | async-done | bytes 4194320 | tf_op jit(solution)/shard_map/all_gather | solution.py:41
  56.4 8.0 %convert_bitcast_fusion = bf16[24,8,128,128]{3,0,2,1:T(8,128)(2,1)} fusion(bf16[8,16,128,128]{3,2,1,0:T(8,128)(2,1)} %all-gather.8.cloned.1.call-done, s32[8,16]{1,0:T(8,128)S(1)} %get-tuple-element.10), kind=kOutput, calls=%fused_computation.3 | convolution fusion | flops 103812096 | bytes 10486272 | tf_op jit(solution)/shard_map/cik,ikab->ciab/dot_general | solution.py:42
  64.4 9.0 %copy.12 = bf16[24,8,128,128]{2,3,1,0:T(8,128)(2,1)} copy(bf16[24,8,128,128]{3,0,2,1:T(8,128)(2,1)} %convert_bitcast_fusion) | data formatting | bytes 12582912 | tf_op jit(solution)/shard_map/convert_element_type | solution.py:44
  73.5 4.6 fusion.53
  78.8 3.5 collective-permute-start.3
  82.3 6.5 collective-permute-start.2
  88.9 3.1 gather_fusion
  94.8 4.9 fusion.33
  100.0 45.1 %all-gather.3 = f32[64,1,128]{2,1,0:T(1,128)S(1)} all-gather(f32[1,1,128]{2,1,0:T(1,128)S(1)} %bitcast.94), channel_id=2, replica_groups=mesh['asset'=64,'rhs'=8] {'asset'}, dimensions={0}, use_global_device_ids=true | all-gather | bytes 33280 | tf_op jit(solution)/shard_map/all_gather | solution.py:47
  145.1 139.1 %psum.21 = f32[128]{0:T(128)S(1)} all-reduce(f32[128]{0:T(128)S(1)} %get-tuple-element.3), channel_id=1, replica_groups=mesh['asset'=64,'rhs'=8] {'asset'}, use_global_device_ids=true, to_apply=%region_3.5 | all-reduce | flops 128 | bytes 1024 | tf_op jit(solution)/shard_map/psum | solution.py:73
  284.6 40.5 %all-gather.4 = f32[64,1,128]{2,1,0:T(1,128)S(1)} all-gather(f32[1,1,128]{2,1,0:T(1,128)S(1)} %bitcast.95), channel_id=3, replica_groups=mesh['asset'=64,'rhs'=8] {'asset'}, dimensions={0}, use_global_device_ids=true | all-gather | bytes 33280 | tf_op jit(solution)/shard_map/all_gather | solution.py:47
  325.4 3.3 collective-permute-start.5
  331.2 5.7 fusion.54
  338.9 7.4 %collective-permute-start.6 = (bf16[8,128,128]{2,1,0:T(8,128)(2,1)S(1)}, bf16[8,128,128]{2,1,0:T(8,128)(2,1)}, u32[]{:S(2)}, u32[]{:S(2)}) collective-permute-start(bf16[8,128,128]{2,1,0:T(8,128)(2,1)S(1)} %get-tuple-element.15), channel_id=1, source_target_pairs={{8,0},{16,8},{24,16},{32,24},{40,32},{48,40},{56,48},{64,56},{72,6... | collective-permute-start | bytes 786440 | tf_op jit(solution)/shard_map/ppermute | solution.py:12
  346.5 3.1 gather_fusion.1
  350.1 4.9 fusion.30
  355.2 143.9 %psum.22 = f32[128]{0:T(128)S(1)} all-reduce(f32[128]{0:T(128)S(1)} %multiply_reduce_fusion.2), channel_id=1, replica_groups=mesh['asset'=64,'rhs'=8] {'asset'}, use_global_device_ids=true, to_apply=%region_7.9 | all-reduce | flops 128 | bytes 1024 | tf_op jit(solution)/shard_map/psum | solution.py:73
  499.4 37.8 %all-gather.5 = f32[64,1,128]{2,1,0:T(1,128)S(1)} all-gather(f32[1,1,128]{2,1,0:T(1,128)S(1)} %bitcast.96), channel_id=4, replica_groups=mesh['asset'=64,'rhs'=8] {'asset'}, dimensions={0}, use_global_device_ids=true | all-gather | bytes 33280 | tf_op jit(solution)/shard_map/all_gather | solution.py:47
  537.3 5.2 collective-permute-start.9
  544.4 5.7 fusion.55
  553.2 6.2 collective-permute-start.10
  563.3 5.0 fusion.27
  568.6 143.9 %psum.23 = f32[128]{0:T(128)S(1)} all-reduce(f32[128]{0:T(128)S(1)} %multiply_reduce_fusion), channel_id=1, replica_groups=mesh['asset'=64,'rhs'=8] {'asset'}, use_global_device_ids=true, to_apply=%region_11.13 | all-reduce | flops 128 | bytes 1024 | tf_op jit(solution)/shard_map/psum | solution.py:73
  (53 shorter events, 26.9 us)
Async XLA Ops:
  7.2 49.3 %all-gather.8.cloned.1.call-start = ((), (), s32[]{:S(2)}) async-start(), calls=%async_computation | async-start | bytes 4718592 | tf_op jit(solution)/shard_map/all_gather | solution.py:41
  11.1 77.8 %collective-permute-start.1 = (bf16[1024,128]{1,0:T(8,128)(2,1)S(1)}, bf16[1024,128]{1,0:T(8,128)(2,1)S(1)}, u32[]{:S(2)}, u32[]{:S(2)}) collective-permute-start(bf16[1024,128]{1,0:T(8,128)(2,1)S(1)} %convert_element_type.49), channel_id=1, source_target_pairs={{8,0},{16,8},{24,16},{32,24},{40,32},{48,40},{56,48},{64,56},{72,6... | collective-permute-start | bytes 786440 | tf_op jit(solution)/shard_map/ppermute | solution.py:23
  24.9 63.9 %collective-permute-start = (bf16[1024,128]{1,0:T(8,128)(2,1)S(1)}, bf16[1024,128]{1,0:T(8,128)(2,1)S(1)}, u32[]{:S(2)}, u32[]{:S(2)}) collective-permute-start(bf16[1024,128]{1,0:T(8,128)(2,1)S(1)} %convert_element_type.49), channel_id=1, source_target_pairs={{0,8},{8,16},{16,24},{24,32},{32,40},{40,48},{48,56},{56,64},{64,7... | collective-permute-start | bytes 786440 | tf_op jit(solution)/shard_map/ppermute | solution.py:22
  78.8 15.1 %collective-permute-start.3 = (bf16[8,128,128]{2,1,0:T(8,128)(2,1)}, bf16[8,128,128]{2,1,0:T(8,128)(2,1)}, u32[]{:S(2)}, u32[]{:S(2)}) collective-permute-start(bf16[8,128,128]{2,1,0:T(8,128)(2,1)} %get-tuple-element.18), channel_id=1, source_target_pairs={{504,0},{0,8},{8,16},{16,24},{24,32},{32,40},{40,48},{48,56},{56,6... | collective-permute-start | bytes 786440 | tf_op jit(solution)/shard_map/ppermute | solution.py:12
  82.3 12.5 %collective-permute-start.2 = (bf16[8,128,128]{2,1,0:T(8,128)(2,1)S(1)}, bf16[8,128,128]{2,1,0:T(8,128)(2,1)}, u32[]{:S(2)}, u32[]{:S(2)}) collective-permute-start(bf16[8,128,128]{2,1,0:T(8,128)(2,1)S(1)} %get-tuple-element.17), channel_id=1, source_target_pairs={{8,0},{16,8},{24,16},{32,24},{40,32},{48,40},{56,48},{64,56},{72,6... | collective-permute-start | bytes 786440 | tf_op jit(solution)/shard_map/ppermute | solution.py:12
  94.8 4.9 copy-start
  94.8 5.0 copy-start.1
  325.4 21.0 %collective-permute-start.5 = (bf16[1024,128]{1,0:T(8,128)(2,1)S(1)}, bf16[1024,128]{1,0:T(8,128)(2,1)S(1)}, u32[]{:S(2)}, u32[]{:S(2)}) collective-permute-start(bf16[1024,128]{1,0:T(8,128)(2,1)S(1)} %get-tuple-element.7), channel_id=1, source_target_pairs={{8,0},{16,8},{24,16},{32,24},{40,32},{48,40},{56,48},{64,56},{72,6... | collective-permute-start | bytes 786440 | tf_op jit(solution)/shard_map/ppermute | solution.py:23
  328.7 17.7 %collective-permute-start.4 = (bf16[1024,128]{1,0:T(8,128)(2,1)S(1)}, bf16[1024,128]{1,0:T(8,128)(2,1)S(1)}, u32[]{:S(2)}, u32[]{:S(2)}) collective-permute-start(bf16[1024,128]{1,0:T(8,128)(2,1)S(1)} %get-tuple-element.7), channel_id=1, source_target_pairs={{0,8},{8,16},{16,24},{24,32},{32,40},{40,48},{48,56},{56,64},{64,7... | collective-permute-start | bytes 786440 | tf_op jit(solution)/shard_map/ppermute | solution.py:22
  337.0 12.6 %collective-permute-start.7 = (bf16[8,128,128]{2,1,0:T(8,128)(2,1)S(1)}, bf16[8,128,128]{2,1,0:T(8,128)(2,1)S(1)}, u32[]{:S(2)}, u32[]{:S(2)}) collective-permute-start(bf16[8,128,128]{2,1,0:T(8,128)(2,1)S(1)} %get-tuple-element.16), channel_id=1, source_target_pairs={{504,0},{0,8},{8,16},{16,24},{24,32},{32,40},{40,48},{48,56},{56,6... | collective-permute-start | bytes 786440 | tf_op jit(solution)/shard_map/ppermute | solution.py:12
  338.9 11.1 %collective-permute-start.6 = (bf16[8,128,128]{2,1,0:T(8,128)(2,1)S(1)}, bf16[8,128,128]{2,1,0:T(8,128)(2,1)}, u32[]{:S(2)}, u32[]{:S(2)}) collective-permute-start(bf16[8,128,128]{2,1,0:T(8,128)(2,1)S(1)} %get-tuple-element.15), channel_id=1, source_target_pairs={{8,0},{16,8},{24,16},{32,24},{40,32},{48,40},{56,48},{64,56},{72,6... | collective-permute-start | bytes 786440 | tf_op jit(solution)/shard_map/ppermute | solution.py:12
  537.3 22.1 %collective-permute-start.9 = (bf16[1024,128]{1,0:T(8,128)(2,1)S(1)}, bf16[1024,128]{1,0:T(8,128)(2,1)S(1)}, u32[]{:S(2)}, u32[]{:S(2)}) collective-permute-start(bf16[1024,128]{1,0:T(8,128)(2,1)S(1)} %fusion.34), channel_id=1, source_target_pairs={{8,0},{16,8},{24,16},{32,24},{40,32},{48,40},{56,48},{64,56},{72,6... | collective-permute-start | bytes 786440 | tf_op jit(solution)/shard_map/ppermute | solution.py:23
  542.5 16.9 %collective-permute-start.8 = (bf16[1024,128]{1,0:T(8,128)(2,1)S(1)}, bf16[1024,128]{1,0:T(8,128)(2,1)S(1)}, u32[]{:S(2)}, u32[]{:S(2)}) collective-permute-start(bf16[1024,128]{1,0:T(8,128)(2,1)S(1)} %fusion.34), channel_id=1, source_target_pairs={{0,8},{8,16},{16,24},{24,32},{32,40},{40,48},{48,56},{56,64},{64,7... | collective-permute-start | bytes 786440 | tf_op jit(solution)/shard_map/ppermute | solution.py:22
  550.2 12.3 %collective-permute-start.11 = (bf16[8,128,128]{2,1,0:T(8,128)(2,1)S(1)}, bf16[8,128,128]{2,1,0:T(8,128)(2,1)}, u32[]{:S(2)}, u32[]{:S(2)}) collective-permute-start(bf16[8,128,128]{2,1,0:T(8,128)(2,1)S(1)} %get-tuple-element.14), channel_id=1, source_target_pairs={{504,0},{0,8},{8,16},{16,24},{24,32},{32,40},{40,48},{48,56},{56,6... | collective-permute-start | bytes 786440 | tf_op jit(solution)/shard_map/ppermute | solution.py:12
  553.2 10.2 %collective-permute-start.10 = (bf16[8,128,128]{2,1,0:T(8,128)(2,1)S(1)}, bf16[8,128,128]{2,1,0:T(8,128)(2,1)}, u32[]{:S(2)}, u32[]{:S(2)}) collective-permute-start(bf16[8,128,128]{2,1,0:T(8,128)(2,1)S(1)} %get-tuple-element.13), channel_id=1, source_target_pairs={{8,0},{16,8},{24,16},{32,24},{40,32},{48,40},{56,48},{64,56},{72,6... | collective-permute-start | bytes 786440 | tf_op jit(solution)/shard_map/ppermute | solution.py:12
Sparse Core Ops, SparseCore 0:
  10.7 45.7 all-gather.7
